TPU v7x, 128 devices: a whole 4x4x4 slice. The times are simulated.
128 devices in a mesh: ha: 16 (over z, y_hi, core), wa: 8 (over x, y_lo).
Axes of the slice: x: 4, y: 4 (y_hi: 2, y_lo: 2; y = y_hi * 2 + y_lo), z: 4, core: 2. Of those that a mesh axis runs over, the one named last changes fastest.
Arguments:
- inputs: bfloat16 [64, 512, 512], P('ha', 'wa'), may hold values from -6 to 6
- grad_out: bfloat16 [64, 512, 512], P('ha', 'wa'), may hold values from -6 to 6
- kernel_one: bfloat16 [27, 64, 64], replicated, may hold values from -0.15625 to 0.15625
- kernel_two: bfloat16 [27, 64, 64], replicated, may hold values from -0.15625 to 0.15625
Outputs:
- grad_inputs: bfloat16 [64, 512, 512], P('ha', 'wa')
- grad_kernel_one: float32 [110592], P(('ha', 'wa'))
- grad_kernel_two: float32 [110592], P(('ha', 'wa'))
All inputs are finite; a program needn't handle non-finite values.
Results may differ from a plain program's by a relative error of at most 0.0049.
Values may be sent and summed in bfloat16 or wider, within the bound.
A program may use at most 64 MiB of HBM per device.

v0:
```python
import functools

import jax
import jax.numpy as jnp
from jax import lax
from jax.experimental import pallas as pl
from jax.experimental.pallas import tpu as pltpu
from jax.sharding import PartitionSpec as P

CH = 64
DEPTH = 8
TAPS = 27
LANES = DEPTH * CH
PADDED = LANES + 2 * CH
QUAD = 4 * CH
WINDOW = 6 * CH
KTOTAL = 9 * WINDOW
MESH = pl.DeviceIdType.MESH
F32 = jnp.float32
BF16 = jnp.bfloat16

root_half = 0.7071067811865476
inv_root_two_pi = 0.3989422804014327


def round_up(value, multiple):
    return -(-value // multiple) * multiple


def kernel(
    sizes,
    x_hbm,
    g_hbm,
    k1_hbm,
    k2_hbm,
    gi_hbm,
    fin_ref,
    xl,
    gl,
    kraw,
    kd,
    w1,
    w2,
    w3,
    esend,
    erecv,
    rowbuf,
    shifted,
    gpl,
    active,
    gout,
    packed,
    piece,
    got,
    total,
    window,
    wgot,
    out_buf,
    local_sem,
    halo_send,
    halo_recv,
    first_send,
    first_recv,
    second_send,
    second_recv,
):
    n_ha, n_wa, rows, cols = sizes
    ha = lax.axis_index("ha")
    wa = lax.axis_index("wa")
    cells = rows * cols
    rows_first = (TAPS * CH) // n_ha
    first_pad = piece.shape[1]
    win_pad = window.shape[1]

    def ha_at(step):
        return lax.rem(ha + (step + n_ha), n_ha)

    def wa_at(step):
        return lax.rem(wa + (step + n_wa), n_wa)

    barrier = pltpu.get_barrier_semaphore()
    peers = [(ha_at(d), wa) for d in range(1, n_ha)]
    peers += [(ha, wa_at(d)) for d in range(1, n_wa)]
    peers += [(ha_at(a), wa_at(b)) for a in (-1, 1) for b in (-1, 1)]
    for peer in peers:
        pl.semaphore_signal(barrier, inc=1, device_id=peer, device_id_type=MESH)

    loads = [
        pltpu.make_async_copy(k1_hbm, kraw.at[0], local_sem.at[0]),
        pltpu.make_async_copy(k2_hbm, kraw.at[1], local_sem.at[1]),
        pltpu.make_async_copy(x_hbm, xl, local_sem.at[2]),
        pltpu.make_async_copy(g_hbm, gl, local_sem.at[3]),
    ]
    for load in loads:
        load.start()

    def edges(field_refs, side):
        start, pick = (0, 0) if side == 0 else (cols - 16, 15)
        ids = lax.broadcasted_iota(jnp.int32, (16, LANES), 0)
        value = jnp.zeros((16, LANES), F32)
        for f, ref in enumerate(field_refs):
            for h in range(rows):
                block = ref[h, start : start + 16, :].astype(F32)
                cell = jnp.broadcast_to(block[pick : pick + 1], (16, LANES))
                value = jnp.where(ids == f * 8 + h, cell, value)
        return value.astype(BF16)

    def exchange(phase, field_refs):
        copies = []
        for f, ref in enumerate(field_refs):
            slot = phase * 2 + f
            for side, row, step in ((0, rows - 1, 1), (1, 0, -1)):
                copies.append(
                    pltpu.make_async_remote_copy(
                        src_ref=ref.at[row],
                        dst_ref=rowbuf.at[slot, side],
                        send_sem=halo_send.at[phase, f * 2 + side],
                        recv_sem=halo_recv.at[phase, f * 2 + side],
                        device_id=(ha_at(step), wa),
                        device_id_type=MESH,
                    )
                )
        for side, wa_step in ((0, -1), (1, 1)):
            for dh in (-1, 0, 1):
                slot = (1 - side) * 3 + 1 - dh
                copies.append(
                    pltpu.make_async_remote_copy(
                        src_ref=esend.at[phase, side],
                        dst_ref=erecv.at[phase, slot],
                        send_sem=halo_send.at[phase, 4 + slot],
                        recv_sem=halo_recv.at[phase, 4 + slot],
                        device_id=(ha_at(dh), wa_at(wa_step)),
                        device_id_type=MESH,
                    )
                )
        for copy in copies:
            copy.start()
        return copies

    def widen(value):
        zeros = jnp.zeros((value.shape[0], PADDED - LANES), F32)
        return pltpu.roll(jnp.concatenate([value, zeros], axis=1), CH, 1)

    low_ok = ha > 0
    high_ok = ha < n_ha - 1
    left_ok = wa > 0
    right_ok = wa < n_wa - 1
    cell_ids = lax.broadcasted_iota(jnp.int32, (cols, PADDED), 0)

    def prepare(phase, f, ref, dst):
        slot = phase * 2 + f
        oks = (low_ok, None, high_ok)
        halo_cells = []
        for side, ok in ((0, left_ok), (1, right_ok)):
            group = []
            for r in range(3):
                value = widen(erecv[phase, side * 3 + r].astype(F32))
                good = ok if oks[r] is None else jnp.logical_and(ok, oks[r])
                group.append(jnp.where(good, value, 0.0))
            halo_cells.append(group)
        for e in range(rows + 2):
            if e == 0:
                value = jnp.where(low_ok, rowbuf[slot, 0].astype(F32), 0.0)
                r, h = 0, rows - 1
            elif e == rows + 1:
                value = jnp.where(high_ok, rowbuf[slot, 1].astype(F32), 0.0)
                r, h = 2, 0
            else:
                value = ref[e - 1].astype(F32)
                r, h = 1, e - 1
            value = widen(value)
            left = halo_cells[0][r][f * 8 + h : f * 8 + h + 1]
            right = halo_cells[1][r][f * 8 + h : f * 8 + h + 1]
            before = jnp.where(
                cell_ids == 0,
                jnp.broadcast_to(left, (cols, PADDED)),
                pltpu.roll(value, 1, 0),
            )
            after = jnp.where(
                cell_ids == cols - 1,
                jnp.broadcast_to(right, (cols, PADDED)),
                pltpu.roll(value, cols - 1, 0),
            )
            shifted[dst, 0, e] = before.astype(BF16)
            shifted[dst, 1, e] = value.astype(BF16)
            shifted[dst, 2, e] = after.astype(BF16)

    lane_low = lax.broadcasted_iota(jnp.int32, (CH, 2 * CH), 1) < CH
    zero_block = jnp.zeros((CH, 2 * CH), BF16)

    def double(which):
        @pl.loop(0, TAPS)
        def _(t):
            block = kraw[which, t].astype(F32)
            kd[which, t] = jnp.concatenate([block, block], axis=1).astype(BF16)

    def build_rows(which, dst):
        @pl.loop(0, 9)
        def _(ab):
            for di in range(6):
                for m in range(2):
                    parts = []
                    for do in (2 * m, 2 * m + 1):
                        c = di - do
                        parts.append(kd[which, ab * 3 + c] if 0 <= c <= 2 else zero_block)
                    start = pl.multiple_of(ab * WINDOW + di * CH, CH)
                    dst[pl.ds(start, CH), m * 128 : m * 128 + 128] = jnp.where(
                        lane_low, parts[0], parts[1]
                    )

    def build_turned(which, dst):
        @pl.loop(0, 9)
        def _(ab):
            for do in range(4):
                for m in range(3):
                    parts = []
                    for di in (2 * m, 2 * m + 1):
                        c = di - do
                        parts.append(
                            kd[which, TAPS - 1 - (ab * 3 + c)] if 0 <= c <= 2 else zero_block
                        )
                    start = pl.multiple_of(ab * WINDOW + m * 128, 128)
                    dst[do * CH : (do + 1) * CH, pl.ds(start, 128)] = jnp.where(
                        lane_low, parts[0], parts[1]
                    )

    loads[2].wait()
    loads[3].wait()
    for side in range(2):
        esend[0, side] = edges((xl, gl), side)
    pl.semaphore_wait(barrier, len(peers))
    halos = exchange(0, (xl, gl))

    loads[0].wait()
    loads[1].wait()
    double(0)
    double(1)
    build_rows(0, w1)
    build_turned(1, w2)
    build_turned(0, w3)

    for copy in halos:
        copy.wait()
    prepare(0, 0, xl, 0)
    prepare(0, 1, gl, 1)

    def stacked(src, q):
        return jnp.concatenate(
            [
                shifted[src, b, a : a + rows, :, q * QUAD : q * QUAD + WINDOW].reshape(
                    cells, WINDOW
                )
                for a in range(3)
                for b in range(3)
            ],
            axis=1,
        )

    def conv(src, q, weights, turned):
        dims = (((1,), (1,)), ((), ())) if turned else (((1,), (0,)), ((), ()))
        return lax.dot_general(stacked(src, q), weights[...], dims, preferred_element_type=F32)

    for q in range(2):
        pre = conv(0, q, w1, False)
        grad_active = conv(1, q, w2, True)
        phi = 0.5 * (1.0 + lax.erf(pre * root_half))
        active[q] = (pre * phi).astype(BF16)
        slope = phi + pre * inv_root_two_pi * jnp.exp(-0.5 * pre * pre)
        grad_pre = (grad_active * slope).astype(BF16)
        gpl[:, :, q * QUAD : (q + 1) * QUAD] = grad_pre.reshape(rows, cols, QUAD)

    for side in range(2):
        esend[1, side] = edges((gpl,), side)
    halos = exchange(1, (gpl,))

    half = lax.broadcasted_iota(jnp.int32, (CH, 128), 1) < CH
    flip_dims = (((0,), (0,)), ((), ()))

    def diagonals(value):
        blocks = [value[d * CH : (d + 1) * CH] for d in range(4)]
        even = [blocks[0][:, i * 128 : i * 128 + 128] + blocks[2][:, (i + 1) * 128 : (i + 1) * 128 + 128] for i in range(2)]
        odd = [blocks[1][:, i * 128 : i * 128 + 128] + blocks[3][:, (i + 1) * 128 : (i + 1) * 128 + 128] for i in range(2)]
        return even, odd

    @pl.loop(0, 9)
    def _(ab):
        a = ab // 3
        b = ab - a * 3
        one = jnp.zeros((QUAD, WINDOW), F32)
        two = jnp.zeros((QUAD, WINDOW), F32)
        for q in range(2):
            lanes = slice(q * QUAD, q * QUAD + WINDOW)
            xw = shifted[0, b, pl.ds(a, rows), :, lanes].reshape(cells, WINDOW)
            gw = shifted[1, 2 - b, pl.ds(2 - a, rows), :, lanes].reshape(cells, WINDOW)
            gp = gpl[:, :, q * QUAD : (q + 1) * QUAD].reshape(cells, QUAD)
            one += lax.dot_general(gp, xw, flip_dims, preferred_element_type=F32)
            two += lax.dot_general(active[q], gw, flip_dims, preferred_element_type=F32)
        even, odd = diagonals(one)
        turn = [pltpu.roll(v, CH, 1) for v in odd]
        first = even[0] + jnp.where(half, turn[0], turn[1])
        second = even[1] + turn[1]
        kernel_one = jnp.concatenate([first.T, second.T[:CH]], axis=0)
        even, odd = diagonals(two)
        turn = [pltpu.roll(v, CH, 1) for v in even]
        third = odd[0] + turn[0]
        mid = even[0] + jnp.where(half, pltpu.roll(odd[0], CH, 1), pltpu.roll(odd[1], CH, 1))
        last = odd[1] + turn[1]
        kernel_two = jnp.concatenate([last, mid, third], axis=0)
        start = pl.multiple_of(ab * 3 * CH, CH)
        packed[pl.ds(start, 3 * CH), :] = jnp.concatenate(
            [kernel_one, kernel_two[:, CH:]], axis=1
        )

    for j in range(n_ha):
        piece[j, 0:rows_first, :] = packed[j * rows_first : (j + 1) * rows_first, :].astype(BF16)
    firsts = []
    for d in range(1, n_ha):
        to = ha_at(d)
        firsts.append(
            pltpu.make_async_remote_copy(
                src_ref=piece.at[to],
                dst_ref=got.at[d],
                send_sem=first_send.at[d],
                recv_sem=first_recv.at[d],
                device_id=(to, wa),
                device_id_type=MESH,
            )
        )
    for copy in firsts:
        copy.start()

    for copy in halos:
        copy.wait()
    prepare(1, 0, gpl, 2)
    for q in range(2):
        value = conv(2, q, w3, True).astype(BF16)
        gout[:, :, q * QUAD : (q + 1) * QUAD] = value.reshape(rows, cols, QUAD)
    store = pltpu.make_async_copy(gout, gi_hbm, local_sem.at[4])
    store.start()

    for copy in firsts:
        copy.wait()
    value = piece[ha].astype(F32)
    for d in range(1, n_ha):
        value += got[d].astype(F32)
    total[...] = value
    starts = [(k * rows_first) // n_wa for k in range(n_wa)]
    for k in range(n_wa):
        count = min(win_pad, first_pad - starts[k])
        window[k, 0:count, :] = total[starts[k] : starts[k] + count, :]
    seconds = []
    for d in range(1, n_wa):
        to = wa_at(d)
        seconds.append(
            pltpu.make_async_remote_copy(
                src_ref=window.at[to],
                dst_ref=wgot.at[d],
                send_sem=second_send.at[d],
                recv_sem=second_recv.at[d],
                device_id=(ha, to),
                device_id_type=MESH,
            )
        )
    for copy in seconds:
        copy.start()
    for copy in seconds:
        copy.wait()
    value = window[wa]
    for d in range(1, n_wa):
        value += wgot[d]
    fin_ref[...] = value
    store.wait()


def shards(sizes, inputs, grad_out, kernel_one, kernel_two):
    n_ha, n_wa, rows, cols = sizes
    rows_first = (TAPS * CH) // n_ha
    first_pad = round_up(rows_first, 16)
    exact = (TAPS * CH * CH) // (n_ha * n_wa)
    win = -(-exact // CH) + (1 if exact % CH else 0)
    win_pad = round_up(win, 8)
    any_spec = pl.BlockSpec(memory_space=pl.ANY)
    dma = pltpu.SemaphoreType.DMA
    grad_inputs, fin = pl.pallas_call(
        functools.partial(kernel, sizes),
        out_shape=(
            jax.ShapeDtypeStruct((rows, cols, LANES), BF16),
            jax.ShapeDtypeStruct((win_pad, 2 * CH), F32),
        ),
        in_specs=[any_spec] * 4,
        out_specs=(any_spec, pl.BlockSpec(memory_space=pltpu.VMEM)),
        scratch_shapes=[
            pltpu.VMEM((rows, cols, LANES), BF16),
            pltpu.VMEM((rows, cols, LANES), BF16),
            pltpu.VMEM((2, TAPS, CH, CH), BF16),
            pltpu.VMEM((2, TAPS, CH, 2 * CH), BF16),
            pltpu.VMEM((KTOTAL, QUAD), BF16),
            pltpu.VMEM((QUAD, KTOTAL), BF16),
            pltpu.VMEM((QUAD, KTOTAL), BF16),
            pltpu.VMEM((2, 2, 16, LANES), BF16),
            pltpu.VMEM((2, 6, 16, LANES), BF16),
            pltpu.VMEM((3, 2, cols, LANES), BF16),
            pltpu.VMEM((3, 3, rows + 2, cols, PADDED), BF16),
            pltpu.VMEM((rows, cols, LANES), BF16),
            pltpu.VMEM((2, rows * cols, QUAD), BF16),
            pltpu.VMEM((rows, cols, LANES), BF16),
            pltpu.VMEM((TAPS * CH, 2 * CH), F32),
            pltpu.VMEM((n_ha, first_pad, 2 * CH), BF16),
            pltpu.VMEM((n_ha, first_pad, 2 * CH), BF16),
            pltpu.VMEM((first_pad, 2 * CH), F32),
            pltpu.VMEM((n_wa, win_pad, 2 * CH), F32),
            pltpu.VMEM((n_wa, win_pad, 2 * CH), F32),
            pltpu.VMEM((8, 128), F32),
            dma((5,)),
            dma((2, 10)),
            dma((2, 10)),
            dma((n_ha,)),
            dma((n_ha,)),
            dma((n_wa,)),
            dma((n_wa,)),
        ],
        compiler_params=pltpu.CompilerParams(
            collective_id=0, has_side_effects=True, vmem_limit_bytes=60 * 1024 * 1024
        ),
    )(inputs, grad_out, kernel_one, kernel_two)
    wa = lax.axis_index("wa")
    begin = (wa * (exact * n_wa)) // n_wa - ((wa * rows_first) // n_wa) * CH
    begin = wa * exact - ((wa * rows_first) // n_wa) * CH

    def cut(lanes):
        flat = fin[:win, lanes].reshape(-1)
        return lax.dynamic_slice(flat, (begin,), (exact,))

    return grad_inputs, cut(slice(0, CH)), cut(slice(CH, 2 * CH))


def solution(mesh):
    n_ha, n_wa = mesh.shape["ha"], mesh.shape["wa"]

    def step(inputs, grad_out, kernel_one, kernel_two):
        rows, cols, _ = inputs.shape
        return shards((n_ha, n_wa, rows, cols), inputs, grad_out, kernel_one, kernel_two)

    return jax.shard_map(
        step,
        mesh=mesh,
        in_specs=(P("ha", "wa", None), P("ha", "wa", None), P(), P()),
        out_specs=(P("ha", "wa", None), P(("ha", "wa")), P(("ha", "wa"))),
        check_vma=False,
    )
```

profile of v0, /device:TPU:1, one launch (start us, length us, event | category | flops | bytes accessed | tf_op | source)
XLA Modules:
  0.0 39.9 jit_solution(9842411650656695413)
XLA Ops:
  0.7 35.2 %shard_map.67 = (bf16[4,64,512]{2,1,0:T(8,128)(2,1)}, f32[16,128]{1,0:T(8,128)}) custom-call(bf16[4,64,512]{2,1,0:T(8,128)(2,1)} %x_hbm.1, bf16[4,64,512]{2,1,0:T(8,128)(2,1)} %g_hbm.1, bf16[27,64,64]{2,1,0:T(8,128)(2,1)} %k1_hbm.1, bf16[27,64,64]{2,1,0:T(8,128)(2,1)} %k2_hbm.1), custom_call_target="tpu_custom_call" | custom-call | tf_op jit(solution)/shard_map/pallas_call | solution.py:384
  35.9 0.8 %fusion = (f32[15,64]{1,0:T(8,128)S(1)}, f32[15,64]{1,0:T(8,128)S(1)}) fusion(f32[16,128]{1,0:T(8,128)} %get-tuple-element.6), kind=kLoop, calls=%fused_computation | loop fusion | bytes 15360 | tf_op jit(solution)/shard_map/slice | solution.py:431
  36.7 0.1 reshape.12
  36.8 0.7 %dynamic_slice.6 = f32[864]{0:T(1024)} dynamic-slice(f32[960]{0:T(1024)S(1)} %reshape.12, s32[]{:T(128)S(6)} %select_n.10), dynamic_slice_sizes={864} | dynamic-slice | bytes 6916 | tf_op jit(solution)/shard_map/dynamic_slice | solution.py:432
  37.5 0.1 reshape.13
  37.5 0.7 %dynamic_slice.7 = f32[864]{0:T(1024)} dynamic-slice(f32[960]{0:T(1024)S(1)} %reshape.13, s32[]{:T(128)S(6)} %select_n.10), dynamic_slice_sizes={864} | dynamic-slice | bytes 6916 | tf_op jit(solution)/shard_map/dynamic_slice | solution.py:432
  38.2 1.7 %copy.8 = bf16[4,64,512]{2,1,0:T(8,128)(2,1)} copy(bf16[4,64,512]{2,1,0:T(8,128)(2,1)} %get-tuple-element.12) | data formatting | bytes 524288
where the time goes:
time: 40.1 us; the launch traced here: 39.9 us
  Pallas kernels  35.2 us (88%)
  local copies, waits for them, and re-layouts  3.99 us (10%)
  between operations  0.66 us (2%)
    pallas_call x1, Pallas kernels, shards(): pl.pallas_call(functools.partial(kernel, sizes), out_shape=(jax.ShapeDtyp...  35.2 us
    unnamed x1, local copies, waits for them, and re-layouts  1.67 us
    dynamic_slice x2, local copies, waits for them, and re-layouts, cut(): return lax.dynamic_slice(flat, (begin,), (exact,))  1.34 us
    slice x1, local copies, waits for them, and re-layouts, cut(): flat = fin[:win, lanes].reshape(-1)  0.85 us

commit v1 on v0

v1 whole, which is shorter than its diff:
```python
import functools

import jax
import jax.numpy as jnp
from jax import lax
from jax.experimental import pallas as pl
from jax.experimental.pallas import tpu as pltpu
from jax.sharding import PartitionSpec as P

CH = 64
DEPTH = 8
TAPS = 27
LANES = DEPTH * CH
PADDED = LANES + 2 * CH
PAIR = 2 * CH
PATCH = 4 * CH
KTOTAL = 3 * 16 * CH
MESH = pl.DeviceIdType.MESH
F32 = jnp.float32
BF16 = jnp.bfloat16

root_half = 0.7071067811865476
inv_root_two_pi = 0.3989422804014327


def round_up(value, multiple):
    return -(-value // multiple) * multiple


def kernel(
    sizes,
    x_hbm,
    g_hbm,
    k1_hbm,
    k2_hbm,
    gi_ref,
    fin_ref,
    xl,
    gl,
    kraw,
    kd,
    w1,
    w2,
    w3,
    esend,
    erecv,
    rowbuf,
    shifted,
    gpl,
    turned,
    sums,
    piece,
    got,
    total,
    window,
    wgot,
    local_sem,
    halo_send,
    halo_recv,
    first_send,
    first_recv,
    second_send,
    second_recv,
):
    n_ha, n_wa, rows, cols = sizes
    ha = lax.axis_index("ha")
    wa = lax.axis_index("wa")
    pairs = rows // 2
    rows_first = (TAPS * CH) // (2 * n_ha)
    exact = (TAPS * CH * CH) // (n_ha * n_wa)

    def wrap(value, size):
        value = jnp.where(value >= size, value - size, value)
        return jnp.where(value < 0, value + size, value)

    def ha_at(step):
        return wrap(ha + step, n_ha)

    def wa_at(step):
        return wrap(wa + step, n_wa)

    barrier = pltpu.get_barrier_semaphore()
    peers = [(ha_at(d), wa) for d in range(1, n_ha)]
    peers += [(ha, wa_at(d)) for d in range(1, n_wa)]
    peers += [(ha_at(a), wa_at(b)) for a in (-1, 1) for b in (-1, 1)]
    loads = [
        pltpu.make_async_copy(x_hbm, xl, local_sem.at[2]),
        pltpu.make_async_copy(g_hbm, gl, local_sem.at[3]),
        pltpu.make_async_copy(k1_hbm, kraw.at[0], local_sem.at[0]),
        pltpu.make_async_copy(k2_hbm, kraw.at[1], local_sem.at[1]),
    ]
    for load in loads:
        load.start()
    for peer in peers:
        pl.semaphore_signal(barrier, inc=1, device_id=peer, device_id_type=MESH)

    def edges(field_refs, side):
        start, pick = (0, 0) if side == 0 else (cols - 16, 15)
        ids = lax.broadcasted_iota(jnp.int32, (16, LANES), 0)
        value = jnp.zeros((16, LANES), F32)
        for f, ref in enumerate(field_refs):
            for h in range(rows):
                block = ref[h, start : start + 16, :].astype(F32)
                cell = jnp.broadcast_to(block[pick : pick + 1], (16, LANES))
                value = jnp.where(ids == f * 8 + h, cell, value)
        return value.astype(BF16)

    def exchange(phase, field_refs):
        copies = []
        for f, ref in enumerate(field_refs):
            slot = phase * 2 + f
            for side, row, step in ((0, rows - 1, 1), (1, 0, -1)):
                copies.append(
                    pltpu.make_async_remote_copy(
                        src_ref=ref.at[row],
                        dst_ref=rowbuf.at[slot, side],
                        send_sem=halo_send.at[phase, f * 2 + side],
                        recv_sem=halo_recv.at[phase, f * 2 + side],
                        device_id=(ha_at(step), wa),
                        device_id_type=MESH,
                    )
                )
        for side, wa_step in ((0, -1), (1, 1)):
            for dh in (-1, 0, 1):
                slot = (1 - side) * 3 + 1 - dh
                copies.append(
                    pltpu.make_async_remote_copy(
                        src_ref=esend.at[phase, side],
                        dst_ref=erecv.at[phase, slot],
                        send_sem=halo_send.at[phase, 4 + slot],
                        recv_sem=halo_recv.at[phase, 4 + slot],
                        device_id=(ha_at(dh), wa_at(wa_step)),
                        device_id_type=MESH,
                    )
                )
        for copy in copies:
            copy.start()
        return copies

    def widen(value):
        zeros = jnp.zeros((value.shape[0], PADDED - LANES), F32)
        return pltpu.roll(jnp.concatenate([value, zeros], axis=1), CH, 1)

    low_ok = ha > 0
    high_ok = ha < n_ha - 1
    left_ok = wa > 0
    right_ok = wa < n_wa - 1
    cell_ids = lax.broadcasted_iota(jnp.int32, (cols, PADDED), 0)
    tile_ids = lax.broadcasted_iota(jnp.int32, (16, PADDED), 0)

    def own_rows(ref, dst):
        for h in range(rows):
            value = widen(ref[h].astype(F32))
            shifted[dst, 0, h + 1] = pltpu.roll(value, 1, 0).astype(BF16)
            shifted[dst, 1, h + 1] = value.astype(BF16)
            shifted[dst, 2, h + 1] = pltpu.roll(value, cols - 1, 0).astype(BF16)

    def finish_rows(phase, f, dst):
        slot = phase * 2 + f
        oks = (low_ok, None, high_ok)
        halo_cells = []
        for side, ok in ((0, left_ok), (1, right_ok)):
            group = []
            for r in range(3):
                value = widen(erecv[phase, side * 3 + r].astype(F32))
                good = ok if oks[r] is None else jnp.logical_and(ok, oks[r])
                group.append(jnp.where(good, value, 0.0))
            halo_cells.append(group)
        for h in range(rows):
            left = halo_cells[0][1][f * 8 + h : f * 8 + h + 1]
            right = halo_cells[1][1][f * 8 + h : f * 8 + h + 1]
            tile = shifted[dst, 0, h + 1, 0:16, :].astype(F32)
            tile = jnp.where(tile_ids == 0, jnp.broadcast_to(left, (16, PADDED)), tile)
            shifted[dst, 0, h + 1, 0:16, :] = tile.astype(BF16)
            tile = shifted[dst, 2, h + 1, cols - 16 : cols, :].astype(F32)
            tile = jnp.where(tile_ids == 15, jnp.broadcast_to(right, (16, PADDED)), tile)
            shifted[dst, 2, h + 1, cols - 16 : cols, :] = tile.astype(BF16)
        for e, side, ok, r, h in ((0, 0, low_ok, 0, rows - 1), (rows + 1, 1, high_ok, 2, 0)):
            value = widen(jnp.where(ok, rowbuf[slot, side].astype(F32), 0.0))
            left = halo_cells[0][r][f * 8 + h : f * 8 + h + 1]
            right = halo_cells[1][r][f * 8 + h : f * 8 + h + 1]
            before = jnp.where(
                cell_ids == 0,
                jnp.broadcast_to(left, (cols, PADDED)),
                pltpu.roll(value, 1, 0),
            )
            after = jnp.where(
                cell_ids == cols - 1,
                jnp.broadcast_to(right, (cols, PADDED)),
                pltpu.roll(value, cols - 1, 0),
            )
            shifted[dst, 0, e] = before.astype(BF16)
            shifted[dst, 1, e] = value.astype(BF16)
            shifted[dst, 2, e] = after.astype(BF16)

    lane_low = lax.broadcasted_iota(jnp.int32, (CH, PAIR), 1) < CH
    zero_block = jnp.zeros((CH, PAIR), BF16)

    def double():
        @pl.loop(0, 9)
        def _(ab):
            for c in range(3):
                for which in range(2):
                    block = kraw[which, ab * 3 + c]
                    kd[which, ab * 3 + c] = jnp.concatenate([block, block], axis=1)

    def tap_block(which, index, c):
        return kd[which, index(c)] if 0 <= c <= 2 else zero_block

    def build_rows(which, dst):
        @pl.loop(0, 3)
        def _(b):
            base = b * 16 * CH
            for di in range(4):
                for a in range(4):
                    if a < 3:
                        index = lambda c: 9 * a + 3 * b + c
                        tile = jnp.where(
                            lane_low,
                            tap_block(which, index, di),
                            tap_block(which, index, di - 1),
                        )
                    else:
                        tile = zero_block
                    here = pl.multiple_of(base + (a * 4 + di) * CH, CH)
                    dst[pl.ds(here, CH), 0:PAIR] = tile
                    here = pl.multiple_of(base + ((a + 1) % 4 * 4 + di) * CH, CH)
                    dst[pl.ds(here, CH), PAIR : 2 * PAIR] = tile

    def build_turned(which, dst):
        @pl.loop(0, 3)
        def _(b):
            base = b * 16 * CH
            for dd in range(2):
                for m in range(2):
                    for a in range(4):
                        if a < 3:
                            index = lambda c: TAPS - 1 - (9 * a + 3 * b + c)
                            tile = jnp.where(
                                lane_low,
                                tap_block(which, index, 2 * m - dd),
                                tap_block(which, index, 2 * m + 1 - dd),
                            )
                        else:
                            tile = zero_block
                        here = pl.multiple_of(base + (a * 4 + 2 * m) * CH, 128)
                        dst[dd * CH : (dd + 1) * CH, pl.ds(here, PAIR)] = tile
                        here = pl.multiple_of(base + ((a + 1) % 4 * 4 + 2 * m) * CH, 128)
                        dst[PAIR + dd * CH : PAIR + (dd + 1) * CH, pl.ds(here, PAIR)] = tile

    loads[0].wait()
    loads[1].wait()
    for side in range(2):
        esend[0, side] = edges((xl, gl), side)
    pl.semaphore_wait(barrier, len(peers))
    halos = exchange(0, (xl, gl))

    loads[2].wait()
    loads[3].wait()
    double()
    build_rows(0, w1)
    build_turned(1, w2)
    build_turned(0, w3)
    own_rows(xl, 0)
    own_rows(gl, 1)

    for copy in halos:
        copy.wait()
    finish_rows(0, 0, 0)
    finish_rows(0, 1, 1)

    def patches(src, b, i, hp):
        return jnp.concatenate(
            [
                shifted[src, b, 2 * hp + i, :, dp * PAIR : dp * PAIR + PATCH]
                for dp in range(DEPTH // 2)
            ],
            axis=0,
        )

    def conv(src, hp, weights, flipped):
        left = jnp.concatenate(
            [patches(src, b, i, hp) for b in range(3) for i in range(4)], axis=1
        )
        dims = (((1,), (1,)), ((), ())) if flipped else (((1,), (0,)), ((), ()))
        return lax.dot_general(left, weights[...], dims, preferred_element_type=F32)

    def spread(dst, hp, value):
        for hh in range(2):
            for dp in range(DEPTH // 2):
                dst[2 * hp + hh, :, dp * PAIR : (dp + 1) * PAIR] = value[
                    dp * cols : (dp + 1) * cols, hh * PAIR : (hh + 1) * PAIR
                ]

    block = cols * (DEPTH // 2)
    for hp in range(pairs):
        pre = conv(0, hp, w1, False)
        grad_active = conv(1, hp, w2, True)
        phi = 0.5 * (1.0 + lax.erf(pre * root_half))
        active = (pre * phi).astype(BF16)
        slope = phi + pre * inv_root_two_pi * jnp.exp(-0.5 * pre * pre)
        grad_pre = (grad_active * slope).astype(BF16)
        spread(gpl, hp, grad_pre)
        turned[0, :, hp * block : (hp + 1) * block] = grad_pre.T
        turned[1, :, hp * block : (hp + 1) * block] = active.T

    for side in range(2):
        esend[1, side] = edges((gpl,), side)
    halos = exchange(1, (gpl,))

    half = lax.broadcasted_iota(jnp.int32, (CH, PAIR), 1) < CH

    def gradients(src, b):
        blocks = []
        for i in range(4):
            right = jnp.concatenate([patches(src, b, i, hp) for hp in range(pairs)], axis=0)
            blocks.append(
                lax.dot_general(
                    turned[src],
                    right,
                    (((1,), (0,)), ((), ())),
                    preferred_element_type=F32,
                )
            )
        for a in range(3):
            low, high = blocks[a], blocks[a + 1]
            even = low[0:CH] + high[PAIR : PAIR + CH]
            odd = low[CH:PAIR] + high[PAIR + CH : 2 * PAIR]
            yield a, even[:, :PAIR], even[:, PAIR:], odd[:, :PAIR], odd[:, PAIR:]

    def send_pieces(which):
        for j in range(n_ha):
            first = sums[which, pl.ds(2 * j * rows_first, rows_first, stride=2), :]
            second = sums[which, pl.ds(2 * j * rows_first + 1, rows_first, stride=2), :]
            value = jnp.where(
                lax.broadcasted_iota(jnp.int32, (rows_first, PAIR), 1) < CH,
                first,
                pltpu.roll(second, CH, 1),
            )
            piece[which, j, 0:rows_first, :] = value.astype(BF16)
        copies = []
        for d in range(1, n_ha):
            to = ha_at(d)
            copies.append(
                pltpu.make_async_remote_copy(
                    src_ref=piece.at[which, to],
                    dst_ref=got.at[which, d],
                    send_sem=first_send.at[which, d],
                    recv_sem=first_recv.at[which, d],
                    device_id=(to, wa),
                    device_id_type=MESH,
                )
            )
        for copy in copies:
            copy.start()
        return copies

    for b in range(3):
        for a, even0, even1, odd0, odd1 in gradients(1, b):
            turn = pltpu.roll(odd1, CH, 1)
            values = (even0 + pltpu.roll(odd0, CH, 1), odd1 + pltpu.roll(even0, CH, 1), even1 + turn)
            for c in range(3):
                start = (TAPS - 1 - (9 * a + 3 * b + c)) * CH
                sums[1, start : start + CH, :] = values[c]
    firsts = [None, send_pieces(1)]
    for b in range(3):
        for a, even0, even1, odd0, odd1 in gradients(0, b):
            turn = pltpu.roll(odd1, CH, 1)
            both = even0 + jnp.where(half, pltpu.roll(odd0, CH, 1), turn)
            start = (9 * a + 3 * b) * CH
            sums[0, start : start + 2 * CH, 0:CH] = both.T
            sums[0, start + 2 * CH : start + 3 * CH, 0:CH] = (even1 + turn).T[0:CH]
    firsts[0] = send_pieces(0)

    own_rows(gpl, 2)
    for copy in halos:
        copy.wait()
    finish_rows(1, 0, 2)
    for hp in range(pairs):
        spread(gi_ref, hp, conv(2, hp, w3, True).astype(BF16))

    starts = [(k * rows_first) // n_wa for k in range(n_wa)]
    span = window.shape[2]
    for which in (1, 0):
        for copy in firsts[which]:
            copy.wait()
        value = piece[which, ha].astype(F32)
        for d in range(1, n_ha):
            value += got[which, d].astype(F32)
        total[...] = value
        for k in range(n_wa):
            window[k, which] = total[starts[k] : starts[k] + span, :]
    seconds = []
    for d in range(1, n_wa):
        to = wa_at(d)
        seconds.append(
            pltpu.make_async_remote_copy(
                src_ref=window.at[to],
                dst_ref=wgot.at[d],
                send_sem=second_send.at[d],
                recv_sem=second_recv.at[d],
                device_id=(ha, to),
                device_id_type=MESH,
            )
        )
    for copy in seconds:
        copy.start()
    for copy in seconds:
        copy.wait()
    value = window[wa]
    for d in range(1, n_wa):
        value += wgot[d]
    fin_ref[...] = value


def finish(sizes, gi_ref, fin_ref, gi_hbm, one_ref, two_ref, sem):
    n_ha, n_wa, rows, cols = sizes
    wa = lax.axis_index("wa")
    exact = (TAPS * CH * CH) // (n_ha * n_wa)
    store = pltpu.make_async_copy(gi_ref, gi_hbm, sem)
    store.start()
    offset = lax.rem(wa * exact, 128)
    count = -(-exact // 128)
    lanes = lax.broadcasted_iota(jnp.int32, (count, 128), 1)
    for which, out in ((0, one_ref), (1, two_ref)):
        value = pltpu.roll(fin_ref[which], 128 - offset, 1)
        value = jnp.where(lanes < 128 - offset, value[0:count], value[1 : count + 1])
        for r in range(count):
            width = min(128, exact - r * 128)
            out[pl.ds(r * 128, width)] = value[r, 0:width]
    store.wait()


def shards(sizes, inputs, grad_out, kernel_one, kernel_two):
    n_ha, n_wa, rows, cols = sizes
    rows_first = (TAPS * CH) // (2 * n_ha)
    exact = (TAPS * CH * CH) // (n_ha * n_wa)
    out_rows = -(-exact // 128)
    span = round_up(out_rows + 1, 8)
    first_pad = round_up(max(rows_first, (n_wa - 1) * rows_first // n_wa + span), 16)
    any_spec = pl.BlockSpec(memory_space=pl.ANY)
    vmem_spec = pl.BlockSpec(memory_space=pltpu.VMEM)
    dma = pltpu.SemaphoreType.DMA
    grad_inputs, fin = pl.pallas_call(
        functools.partial(kernel, sizes),
        out_shape=(
            pltpu.VMEM((rows, cols, LANES), BF16),
            pltpu.VMEM((2, span, 128), F32),
        ),
        in_specs=[pl.BlockSpec(memory_space=pltpu.HBM)] * 4,
        out_specs=(vmem_spec, vmem_spec),
        scratch_shapes=[
            pltpu.VMEM((rows, cols, LANES), BF16),
            pltpu.VMEM((rows, cols, LANES), BF16),
            pltpu.VMEM((2, TAPS, CH, CH), BF16),
            pltpu.VMEM((2, TAPS, CH, PAIR), BF16),
            pltpu.VMEM((KTOTAL, PATCH), BF16),
            pltpu.VMEM((PATCH, KTOTAL), BF16),
            pltpu.VMEM((PATCH, KTOTAL), BF16),
            pltpu.VMEM((2, 2, 16, LANES), BF16),
            pltpu.VMEM((2, 6, 16, LANES), BF16),
            pltpu.VMEM((3, 2, cols, LANES), BF16),
            pltpu.VMEM((3, 3, rows + 2, cols, PADDED), BF16),
            pltpu.VMEM((rows, cols, LANES), BF16),
            pltpu.VMEM((2, PATCH, rows * cols * 2), BF16),
            pltpu.VMEM((2, TAPS * CH, PAIR), F32),
            pltpu.VMEM((2, n_ha, first_pad, 128), BF16),
            pltpu.VMEM((2, n_ha, first_pad, 128), BF16),
            pltpu.VMEM((first_pad, 128), F32),
            pltpu.VMEM((n_wa, 2, span, 128), F32),
            pltpu.VMEM((n_wa, 2, span, 128), F32),
            dma((4,)),
            dma((2, 10)),
            dma((2, 10)),
            dma((2, n_ha)),
            dma((2, n_ha)),
            dma((n_wa,)),
            dma((n_wa,)),
        ],
        compiler_params=pltpu.CompilerParams(
            collective_id=0, has_side_effects=True, vmem_limit_bytes=65024 * 1024
        ),
    )(inputs, grad_out, kernel_one, kernel_two)
    return pl.pallas_call(
        functools.partial(finish, sizes),
        out_shape=(
            jax.ShapeDtypeStruct((rows, cols, LANES), BF16),
            jax.ShapeDtypeStruct((exact,), F32),
            jax.ShapeDtypeStruct((exact,), F32),
        ),
        in_specs=[vmem_spec, vmem_spec],
        out_specs=(any_spec, vmem_spec, vmem_spec),
        scratch_shapes=[dma],
        compiler_params=pltpu.CompilerParams(vmem_limit_bytes=8 * 1024 * 1024),
    )(grad_inputs, fin)


def solution(mesh):
    n_ha, n_wa = mesh.shape["ha"], mesh.shape["wa"]

    def step(inputs, grad_out, kernel_one, kernel_two):
        rows, cols, _ = inputs.shape
        return shards((n_ha, n_wa, rows, cols), inputs, grad_out, kernel_one, kernel_two)

    return jax.shard_map(
        step,
        mesh=mesh,
        in_specs=(P("ha", "wa", None), P("ha", "wa", None), P(), P()),
        out_specs=(P("ha", "wa", None), P(("ha", "wa")), P(("ha", "wa"))),
        check_vma=False,
    )
```

time: 40.1 us -> 34.8 us (0.87)
  local copies, waits for them, and re-layouts: 3.99 us -> 0 us
  Pallas kernels: 35.2 us -> 34 us
    unnamed x1 -> x0, local copies, waits for them, and re-layouts: 1.67 us -> none
    dynamic_slice x2 -> x0, local copies, waits for them, and re-layouts: 1.34 us -> none  [cut(): return lax.dynamic_slice(flat, (begin,), (exact,))]
    pallas_call x1 -> x2, Pallas kernels: 35.2 us -> 34 us  [the longest x1 32.7 us: shards(): pl.pallas_call(functools.partial(kernel, sizes), out_shape=(pltpu.VMEM((r...]
    slice x1 -> x0, local copies, waits for them, and re-layouts: 0.85 us -> none  [cut(): flat = fin[:win, lanes].reshape(-1)]
where the time goes in v1:
time: 34.8 us; the launch traced here: 34.7 us
  Pallas kernels  34 us (98%)
  between operations  0.64 us (2%)
    pallas_call x1, Pallas kernels, shards(): pl.pallas_call(functools.partial(kernel, sizes), out_shape=(pltpu.VMEM((r...  32.7 us
    pallas_call x1, Pallas kernels, shards(): pl.pallas_call(functools.partial(finish, sizes), out_shape=(jax.ShapeDtyp...  1.3 us

profile of v1, /device:TPU:1, one launch (start us, length us, event | category | flops | bytes accessed | tf_op | source)
XLA Modules:
  0.0 34.7 jit_solution(8440599277177115843)
XLA Ops:
  0.6 32.7 %shard_map.67 = (bf16[4,64,512]{2,1,0:T(8,128)(2,1)S(1)}, f32[2,8,128]{2,1,0:T(8,128)S(1)}) custom-call(bf16[4,64,512]{2,1,0:T(8,128)(2,1)} %x_hbm.1, bf16[4,64,512]{2,1,0:T(8,128)(2,1)} %g_hbm.1, bf16[27,64,64]{2,1,0:T(8,128)(2,1)} %k1_hbm.1, bf16[27,64,64]{2,1,0:T(8,128)(2,1)} %k2_hbm.1), custom_call_target="tpu_custom_call" | custom-call | tf_op jit(solution)/shard_map/pallas_call | solution.py:444
  33.4 1.3 %shard_map.68 = (bf16[4,64,512]{2,1,0:T(8,128)(2,1)}, f32[864]{0:T(1024)}, f32[864]{0:T(1024)}) custom-call(bf16[4,64,512]{2,1,0:T(8,128)(2,1)S(1)} %get-tuple-element.5.gi_ref, f32[2,8,128]{2,1,0:T(8,128)S(1)} %get-tuple-element.6.fin_ref), custom_call_target="tpu_custom_call" | custom-call | tf_op jit(solution)/shard_map/pallas_call | solution.py:484

commit v2 on v1

--- a/solution.py
+++ b/solution.py
@@ -47,20 +47,25 @@
     rowbuf,
     shifted,
     gpl,
+    slopes,
     turned,
     sums,
     piece,
     got,
+    along,
+    along_got,
     total,
     window,
     wgot,
     local_sem,
     halo_send,
     halo_recv,
-    first_send,
-    first_recv,
-    second_send,
-    second_recv,
+    core_send,
+    core_recv,
+    z_send,
+    z_recv,
+    last_send,
+    last_recv,
 ):
     n_ha, n_wa, rows, cols = sizes
     ha = lax.axis_index("ha")
@@ -79,10 +84,19 @@
     def wa_at(step):
         return wrap(wa + step, n_wa)
 
+    n_z = n_ha // 4
+    core = lax.rem(ha, 2)
+    upper = lax.rem(lax.div(ha, 2), 2)
+    z_here = lax.div(ha, 4)
+    other_core = ha + 1 - 2 * core
+    other_upper = ha + 2 - 4 * upper
+
     barrier = pltpu.get_barrier_semaphore()
-    peers = [(ha_at(d), wa) for d in range(1, n_ha)]
+    peers = [(ha_at(a), wa) for a in (-1, 1)]
+    peers += [(ha_at(a), wa_at(b)) for a in (-1, 1) for b in (-1, 1)]
     peers += [(ha, wa_at(d)) for d in range(1, n_wa)]
-    peers += [(ha_at(a), wa_at(b)) for a in (-1, 1) for b in (-1, 1)]
+    peers += [(other_upper, wa_at(d)) for d in range(n_wa)]
+    peers += [(ha_at(4 * d), wa) for d in range(1, n_z)]
     loads = [
         pltpu.make_async_copy(x_hbm, xl, local_sem.at[2]),
         pltpu.make_async_copy(g_hbm, gl, local_sem.at[3]),
@@ -94,6 +108,8 @@
     for peer in peers:
         pl.semaphore_signal(barrier, inc=1, device_id=peer, device_id_type=MESH)
 
+    sent = []
+
     def edges(field_refs, side):
         start, pick = (0, 0) if side == 0 else (cols - 16, 15)
         ids = lax.broadcasted_iota(jnp.int32, (16, LANES), 0)
@@ -106,11 +122,12 @@
         return value.astype(BF16)
 
     def exchange(phase, field_refs):
-        copies = []
+        rows_of = []
         for f, ref in enumerate(field_refs):
             slot = phase * 2 + f
+            group = []
             for side, row, step in ((0, rows - 1, 1), (1, 0, -1)):
-                copies.append(
+                group.append(
                     pltpu.make_async_remote_copy(
                         src_ref=ref.at[row],
                         dst_ref=rowbuf.at[slot, side],
@@ -120,10 +137,12 @@
                         device_id_type=MESH,
                     )
                 )
+            rows_of.append(group)
+        corners = []
         for side, wa_step in ((0, -1), (1, 1)):
             for dh in (-1, 0, 1):
                 slot = (1 - side) * 3 + 1 - dh
-                copies.append(
+                corners.append(
                     pltpu.make_async_remote_copy(
                         src_ref=esend.at[phase, side],
                         dst_ref=erecv.at[phase, slot],
@@ -133,9 +152,15 @@
                         device_id_type=MESH,
                     )
                 )
-        for copy in copies:
+        for copy in rows_of[0] + corners:
             copy.start()
-        return copies
+        for group in rows_of[1:]:
+            for copy in group:
+                copy.start()
+        sent.extend(corners)
+        for group in rows_of:
+            sent.extend(group)
+        return corners, rows_of
 
     def widen(value):
         zeros = jnp.zeros((value.shape[0], PADDED - LANES), F32)
@@ -253,7 +278,7 @@
     for side in range(2):
         esend[0, side] = edges((xl, gl), side)
     pl.semaphore_wait(barrier, len(peers))
-    halos = exchange(0, (xl, gl))
+    corners, row_copies = exchange(0, (xl, gl))
 
     loads[2].wait()
     loads[3].wait()
@@ -264,10 +289,9 @@
     own_rows(xl, 0)
     own_rows(gl, 1)
 
-    for copy in halos:
-        copy.wait()
+    for copy in corners + row_copies[0]:
+        copy.wait_recv()
     finish_rows(0, 0, 0)
-    finish_rows(0, 1, 1)
 
     def patches(src, b, i, hp):
         return jnp.concatenate(
@@ -295,18 +319,20 @@
     block = cols * (DEPTH // 2)
     for hp in range(pairs):
         pre = conv(0, hp, w1, False)
-        grad_active = conv(1, hp, w2, True)
         phi = 0.5 * (1.0 + lax.erf(pre * root_half))
-        active = (pre * phi).astype(BF16)
-        slope = phi + pre * inv_root_two_pi * jnp.exp(-0.5 * pre * pre)
-        grad_pre = (grad_active * slope).astype(BF16)
+        turned[1, :, hp * block : (hp + 1) * block] = (pre * phi).astype(BF16).T
+        slopes[hp] = phi + pre * inv_root_two_pi * jnp.exp(-0.5 * pre * pre)
+    for copy in row_copies[1]:
+        copy.wait_recv()
+    finish_rows(0, 1, 1)
+    for hp in range(pairs):
+        grad_pre = (conv(1, hp, w2, True) * slopes[hp]).astype(BF16)
         spread(gpl, hp, grad_pre)
         turned[0, :, hp * block : (hp + 1) * block] = grad_pre.T
-        turned[1, :, hp * block : (hp + 1) * block] = active.T
 
     for side in range(2):
         esend[1, side] = edges((gpl,), side)
-    halos = exchange(1, (gpl,))
+    corners, row_copies = exchange(1, (gpl,))
 
     half = lax.broadcasted_iota(jnp.int32, (CH, PAIR), 1) < CH
 
@@ -328,7 +354,7 @@
             odd = low[CH:PAIR] + high[PAIR + CH : 2 * PAIR]
             yield a, even[:, :PAIR], even[:, PAIR:], odd[:, :PAIR], odd[:, PAIR:]
 
-    def send_pieces(which):
+    def send_to_core(which):
         for j in range(n_ha):
             first = sums[which, pl.ds(2 * j * rows_first, rows_first, stride=2), :]
             second = sums[which, pl.ds(2 * j * rows_first + 1, rows_first, stride=2), :]
@@ -337,22 +363,39 @@
                 first,
                 pltpu.roll(second, CH, 1),
             )
-            piece[which, j, 0:rows_first, :] = value.astype(BF16)
+            piece[which, j % 2, j // 2, 0:rows_first, :] = value.astype(BF16)
+        copy = pltpu.make_async_remote_copy(
+            src_ref=piece.at[which, 1 - core],
+            dst_ref=got.at[which],
+            send_sem=core_send.at[which],
+            recv_sem=core_recv.at[which],
+            device_id=(other_core, wa),
+            device_id_type=MESH,
+        )
+        copy.start()
+        sent.append(copy)
+        return copy
+
+    def send_along_z(which, arrival):
+        arrival.wait_recv()
+        for t in range(n_ha // 2):
+            value = piece[which, core, t].astype(F32) + got[which, t].astype(F32)
+            along[which, t // 2, t % 2] = value.astype(BF16)
         copies = []
-        for d in range(1, n_ha):
-            to = ha_at(d)
+        for d in range(1, n_z):
             copies.append(
                 pltpu.make_async_remote_copy(
-                    src_ref=piece.at[which, to],
-                    dst_ref=got.at[which, d],
-                    send_sem=first_send.at[which, d],
-                    recv_sem=first_recv.at[which, d],
-                    device_id=(to, wa),
+                    src_ref=along.at[which, wrap(z_here + d, n_z)],
+                    dst_ref=along_got.at[which, d],
+                    send_sem=z_send.at[which, d],
+                    recv_sem=z_recv.at[which, d],
+                    device_id=(ha_at(4 * d), wa),
                     device_id_type=MESH,
                 )
             )
         for copy in copies:
             copy.start()
+        sent.extend(copies)
         return copies
 
     for b in range(3):
@@ -362,7 +405,8 @@
             for c in range(3):
                 start = (TAPS - 1 - (9 * a + 3 * b + c)) * CH
                 sums[1, start : start + CH, :] = values[c]
-    firsts = [None, send_pieces(1)]
+    arrivals = [None, send_to_core(1)]
+    z_copies = [None, None]
     for b in range(3):
         for a, even0, even1, odd0, odd1 in gradients(0, b):
             turn = pltpu.roll(odd1, CH, 1)
@@ -370,47 +414,59 @@
             start = (9 * a + 3 * b) * CH
             sums[0, start : start + 2 * CH, 0:CH] = both.T
             sums[0, start + 2 * CH : start + 3 * CH, 0:CH] = (even1 + turn).T[0:CH]
-    firsts[0] = send_pieces(0)
+        if b == 1:
+            z_copies[1] = send_along_z(1, arrivals[1])
+    arrivals[0] = send_to_core(0)
 
     own_rows(gpl, 2)
-    for copy in halos:
-        copy.wait()
+    z_copies[0] = send_along_z(0, arrivals[0])
+    for copy in corners + row_copies[0]:
+        copy.wait_recv()
     finish_rows(1, 0, 2)
     for hp in range(pairs):
         spread(gi_ref, hp, conv(2, hp, w3, True).astype(BF16))
 
     starts = [(k * rows_first) // n_wa for k in range(n_wa)]
-    span = window.shape[2]
+    span = window.shape[3]
     for which in (1, 0):
-        for copy in firsts[which]:
-            copy.wait()
-        value = piece[which, ha].astype(F32)
-        for d in range(1, n_ha):
-            value += got[which, d].astype(F32)
-        total[...] = value
-        for k in range(n_wa):
-            window[k, which] = total[starts[k] : starts[k] + span, :]
-    seconds = []
-    for d in range(1, n_wa):
-        to = wa_at(d)
-        seconds.append(
-            pltpu.make_async_remote_copy(
-                src_ref=window.at[to],
-                dst_ref=wgot.at[d],
-                send_sem=second_send.at[d],
-                recv_sem=second_recv.at[d],
-                device_id=(ha, to),
-                device_id_type=MESH,
+        for copy in z_copies[which]:
+            copy.wait_recv()
+        for u in range(2):
+            value = along[which, z_here, u].astype(F32)
+            for d in range(1, n_z):
+                value += along_got[which, d, u].astype(F32)
+            total[which, u] = value
+            for k in range(n_wa):
+                window[u, k, which] = total[which, u, starts[k] : starts[k] + span, :]
+    lasts = []
+    for step in range(2):
+        up = upper if step == 0 else 1 - upper
+        for d in range(n_wa):
+            if step == 0 and d == 0:
+                continue
+            to = wa_at(d)
+            lasts.append(
+                pltpu.make_async_remote_copy(
+                    src_ref=window.at[up, to],
+                    dst_ref=wgot.at[step, d],
+                    send_sem=last_send.at[step, d],
+                    recv_sem=last_recv.at[step, d],
+                    device_id=(ha if step == 0 else other_upper, to),
+                    device_id_type=MESH,
+                )
             )
-        )
-    for copy in seconds:
+    for copy in lasts:
         copy.start()
-    for copy in seconds:
-        copy.wait()
-    value = window[wa]
-    for d in range(1, n_wa):
-        value += wgot[d]
+    for copy in lasts:
+        copy.wait_recv()
+    value = window[upper, wa]
+    for step in range(2):
+        for d in range(n_wa):
+            if step or d:
+                value += wgot[step, d]
     fin_ref[...] = value
+    for copy in sent + lasts:
+        copy.wait_send()
 
 
 def finish(sizes, gi_ref, fin_ref, gi_hbm, one_ref, two_ref, sem):
@@ -462,20 +518,25 @@
             pltpu.VMEM((3, 2, cols, LANES), BF16),
             pltpu.VMEM((3, 3, rows + 2, cols, PADDED), BF16),
             pltpu.VMEM((rows, cols, LANES), BF16),
+            pltpu.VMEM((rows // 2, cols * DEPTH // 2, PATCH), F32),
             pltpu.VMEM((2, PATCH, rows * cols * 2), BF16),
             pltpu.VMEM((2, TAPS * CH, PAIR), F32),
-            pltpu.VMEM((2, n_ha, first_pad, 128), BF16),
-            pltpu.VMEM((2, n_ha, first_pad, 128), BF16),
-            pltpu.VMEM((first_pad, 128), F32),
-            pltpu.VMEM((n_wa, 2, span, 128), F32),
-            pltpu.VMEM((n_wa, 2, span, 128), F32),
+            pltpu.VMEM((2, 2, n_ha // 2, first_pad, 128), BF16),
+            pltpu.VMEM((2, n_ha // 2, first_pad, 128), BF16),
+            pltpu.VMEM((2, n_ha // 4, 2, first_pad, 128), BF16),
+            pltpu.VMEM((2, n_ha // 4, 2, first_pad, 128), BF16),
+            pltpu.VMEM((2, 2, first_pad, 128), F32),
+            pltpu.VMEM((2, n_wa, 2, span, 128), F32),
+            pltpu.VMEM((2, n_wa, 2, span, 128), F32),
             dma((4,)),
             dma((2, 10)),
             dma((2, 10)),
-            dma((2, n_ha)),
-            dma((2, n_ha)),
-            dma((n_wa,)),
-            dma((n_wa,)),
+            dma((2,)),
+            dma((2,)),
+            dma((2, n_ha // 4)),
+            dma((2, n_ha // 4)),
+            dma((2, n_wa)),
+            dma((2, n_wa)),
         ],
         compiler_params=pltpu.CompilerParams(
             collective_id=0, has_side_effects=True, vmem_limit_bytes=65024 * 1024

time: 34.8 us -> 32.9 us (0.945)
  Pallas kernels: 34 us -> 32 us
    pallas_call x1, Pallas kernels: 32.7 us -> 30.7 us  [shards(): pl.pallas_call(functools.partial(kernel, sizes), out_shape=(pltpu.VMEM((r...]
where the time goes in v2:
time: 32.9 us; the launch traced here: 32.6 us
  Pallas kernels  32 us (97%)
  between operations  0.64 us (2%)
    pallas_call x1, Pallas kernels, shards(): pl.pallas_call(functools.partial(kernel, sizes), out_shape=(pltpu.VMEM((r...  30.7 us
    pallas_call x1, Pallas kernels, shards(): pl.pallas_call(functools.partial(finish, sizes), out_shape=(jax.ShapeDtyp...  1.3 us

profile of v2, /device:TPU:1, one launch (start us, length us, event | category | flops | bytes accessed | tf_op | source)
XLA Modules:
  0.0 32.6 jit_solution(16503392312460011953)
XLA Ops:
  0.6 30.7 %shard_map.67 = (bf16[4,64,512]{2,1,0:T(8,128)(2,1)S(1)}, f32[2,8,128]{2,1,0:T(8,128)S(1)}) custom-call(bf16[4,64,512]{2,1,0:T(8,128)(2,1)} %x_hbm.1, bf16[4,64,512]{2,1,0:T(8,128)(2,1)} %g_hbm.1, bf16[27,64,64]{2,1,0:T(8,128)(2,1)} %k1_hbm.1, bf16[27,64,64]{2,1,0:T(8,128)(2,1)} %k2_hbm.1), custom_call_target="tpu_custom_call" | custom-call | tf_op jit(solution)/shard_map/pallas_call | solution.py:500
  31.3 1.3 %shard_map.68 = (bf16[4,64,512]{2,1,0:T(8,128)(2,1)}, f32[864]{0:T(1024)}, f32[864]{0:T(1024)}) custom-call(bf16[4,64,512]{2,1,0:T(8,128)(2,1)S(1)} %get-tuple-element.5.gi_ref, f32[2,8,128]{2,1,0:T(8,128)S(1)} %get-tuple-element.6.fin_ref), custom_call_target="tpu_custom_call" | custom-call | tf_op jit(solution)/shard_map/pallas_call | solution.py:545

commit v3 on v2

--- a/solution.py
+++ b/solution.py
@@ -16,6 +16,7 @@
 PATCH = 4 * CH
 KTOTAL = 3 * 16 * CH
 MESH = pl.DeviceIdType.MESH
+SENT_AFTER = 0
 F32 = jnp.float32
 BF16 = jnp.bfloat16
 
@@ -47,7 +48,7 @@
     rowbuf,
     shifted,
     gpl,
-    slopes,
+    held,
     turned,
     sums,
     piece,
@@ -93,8 +94,9 @@
 
     barrier = pltpu.get_barrier_semaphore()
     peers = [(ha_at(a), wa) for a in (-1, 1)]
+    peers += [(ha, wa_at(d)) for d in (-1, 1)[: n_wa - 1]]
     peers += [(ha_at(a), wa_at(b)) for a in (-1, 1) for b in (-1, 1)]
-    peers += [(ha, wa_at(d)) for d in range(1, n_wa)]
+    peers += [(ha, wa_at(d)) for d in range(2, n_wa - 1)]
     peers += [(other_upper, wa_at(d)) for d in range(n_wa)]
     peers += [(ha_at(4 * d), wa) for d in range(1, n_z)]
     loads = [
@@ -103,9 +105,11 @@
         pltpu.make_async_copy(k1_hbm, kraw.at[0], local_sem.at[0]),
         pltpu.make_async_copy(k2_hbm, kraw.at[1], local_sem.at[1]),
     ]
+    for peer in peers[:8]:
+        pl.semaphore_signal(barrier, inc=1, device_id=peer, device_id_type=MESH)
     for load in loads:
         load.start()
-    for peer in peers:
+    for peer in peers[8:]:
         pl.semaphore_signal(barrier, inc=1, device_id=peer, device_id_type=MESH)
 
     sent = []
@@ -152,15 +156,13 @@
                         device_id_type=MESH,
                     )
                 )
-        for copy in rows_of[0] + corners:
-            copy.start()
-        for group in rows_of[1:]:
+        beside = [corners[1], corners[4]]
+        corners = [corners[i] for i in (0, 2, 3, 5)]
+        for group in [beside, rows_of[0], corners] + rows_of[1:]:
             for copy in group:
                 copy.start()
-        sent.extend(corners)
-        for group in rows_of:
             sent.extend(group)
-        return corners, rows_of
+        return beside, corners, rows_of
 
     def widen(value):
         zeros = jnp.zeros((value.shape[0], PADDED - LANES), F32)
@@ -180,30 +182,30 @@
             shifted[dst, 1, h + 1] = value.astype(BF16)
             shifted[dst, 2, h + 1] = pltpu.roll(value, cols - 1, 0).astype(BF16)
 
-    def finish_rows(phase, f, dst):
-        slot = phase * 2 + f
-        oks = (low_ok, None, high_ok)
-        halo_cells = []
-        for side, ok in ((0, left_ok), (1, right_ok)):
-            group = []
-            for r in range(3):
-                value = widen(erecv[phase, side * 3 + r].astype(F32))
-                good = ok if oks[r] is None else jnp.logical_and(ok, oks[r])
-                group.append(jnp.where(good, value, 0.0))
-            halo_cells.append(group)
+    def halo_cells(phase, side, r):
+        ok = (left_ok, right_ok)[side]
+        if r != 1:
+            ok = jnp.logical_and(ok, (low_ok, None, high_ok)[r])
+        return jnp.where(ok, widen(erecv[phase, side * 3 + r].astype(F32)), 0.0)
+
+    def finish_own(phase, f, dst):
+        sides = [halo_cells(phase, side, 1) for side in range(2)]
         for h in range(rows):
-            left = halo_cells[0][1][f * 8 + h : f * 8 + h + 1]
-            right = halo_cells[1][1][f * 8 + h : f * 8 + h + 1]
+            left = sides[0][f * 8 + h : f * 8 + h + 1]
+            right = sides[1][f * 8 + h : f * 8 + h + 1]
             tile = shifted[dst, 0, h + 1, 0:16, :].astype(F32)
             tile = jnp.where(tile_ids == 0, jnp.broadcast_to(left, (16, PADDED)), tile)
             shifted[dst, 0, h + 1, 0:16, :] = tile.astype(BF16)
             tile = shifted[dst, 2, h + 1, cols - 16 : cols, :].astype(F32)
             tile = jnp.where(tile_ids == 15, jnp.broadcast_to(right, (16, PADDED)), tile)
             shifted[dst, 2, h + 1, cols - 16 : cols, :] = tile.astype(BF16)
+
+    def outer_rows(phase, f, dst):
+        slot = phase * 2 + f
         for e, side, ok, r, h in ((0, 0, low_ok, 0, rows - 1), (rows + 1, 1, high_ok, 2, 0)):
             value = widen(jnp.where(ok, rowbuf[slot, side].astype(F32), 0.0))
-            left = halo_cells[0][r][f * 8 + h : f * 8 + h + 1]
-            right = halo_cells[1][r][f * 8 + h : f * 8 + h + 1]
+            left = halo_cells(phase, 0, r)[f * 8 + h : f * 8 + h + 1]
+            right = halo_cells(phase, 1, r)[f * 8 + h : f * 8 + h + 1]
             before = jnp.where(
                 cell_ids == 0,
                 jnp.broadcast_to(left, (cols, PADDED)),
@@ -278,7 +280,7 @@
     for side in range(2):
         esend[0, side] = edges((xl, gl), side)
     pl.semaphore_wait(barrier, len(peers))
-    corners, row_copies = exchange(0, (xl, gl))
+    beside, corners, row_copies = exchange(0, (xl, gl))
 
     loads[2].wait()
     loads[3].wait()
@@ -289,9 +291,10 @@
     own_rows(xl, 0)
     own_rows(gl, 1)
 
-    for copy in corners + row_copies[0]:
+    for copy in beside:
         copy.wait_recv()
-    finish_rows(0, 0, 0)
+    finish_own(0, 0, 0)
+    finish_own(0, 1, 1)
 
     def patches(src, b, i, hp):
         return jnp.concatenate(
@@ -302,12 +305,23 @@
             axis=0,
         )
 
-    def conv(src, hp, weights, flipped):
-        left = jnp.concatenate(
-            [patches(src, b, i, hp) for b in range(3) for i in range(4)], axis=1
-        )
-        dims = (((1,), (1,)), ((), ())) if flipped else (((1,), (0,)), ((), ()))
-        return lax.dot_general(left, weights[...], dims, preferred_element_type=F32)
+    def inner(hp):
+        return [i for i in range(4) if 0 < 2 * hp + i < rows + 1]
+
+    def outer(hp):
+        return [i for i in range(4) if i not in inner(hp)]
+
+    def conv(src, hp, weights, flipped, window_rows):
+        spots = [(b, i) for b in range(3) for i in window_rows]
+        left = jnp.concatenate([patches(src, b, i, hp) for b, i in spots], axis=1)
+        parts = [slice((b * 4 + i) * PATCH, (b * 4 + i + 1) * PATCH) for b, i in spots]
+        if flipped:
+            right = jnp.concatenate([weights[:, part] for part in parts], axis=1)
+            dims = (((1,), (1,)), ((), ()))
+        else:
+            right = jnp.concatenate([weights[part, :] for part in parts], axis=0)
+            dims = (((1,), (0,)), ((), ()))
+        return lax.dot_general(left, right, dims, preferred_element_type=F32)
 
     def spread(dst, hp, value):
         for hh in range(2):
@@ -318,21 +332,24 @@
 
     block = cols * (DEPTH // 2)
     for hp in range(pairs):
-        pre = conv(0, hp, w1, False)
+        held[0, hp] = conv(0, hp, w1, False, inner(hp))
+        held[1, hp] = conv(1, hp, w2, True, inner(hp))
+    for copy in row_copies[0] + corners:
+        copy.wait_recv()
+    outer_rows(0, 0, 0)
+    for hp in range(pairs):
+        pre = held[0, hp] + conv(0, hp, w1, False, outer(hp))
         phi = 0.5 * (1.0 + lax.erf(pre * root_half))
         turned[1, :, hp * block : (hp + 1) * block] = (pre * phi).astype(BF16).T
-        slopes[hp] = phi + pre * inv_root_two_pi * jnp.exp(-0.5 * pre * pre)
+        held[0, hp] = phi + pre * inv_root_two_pi * jnp.exp(-0.5 * pre * pre)
     for copy in row_copies[1]:
         copy.wait_recv()
-    finish_rows(0, 1, 1)
+    outer_rows(0, 1, 1)
     for hp in range(pairs):
-        grad_pre = (conv(1, hp, w2, True) * slopes[hp]).astype(BF16)
+        grad_active = held[1, hp] + conv(1, hp, w2, True, outer(hp))
+        grad_pre = (grad_active * held[0, hp]).astype(BF16)
         spread(gpl, hp, grad_pre)
         turned[0, :, hp * block : (hp + 1) * block] = grad_pre.T
-
-    for side in range(2):
-        esend[1, side] = edges((gpl,), side)
-    corners, row_copies = exchange(1, (gpl,))
 
     half = lax.broadcasted_iota(jnp.int32, (CH, PAIR), 1) < CH
 
@@ -405,6 +422,10 @@
             for c in range(3):
                 start = (TAPS - 1 - (9 * a + 3 * b + c)) * CH
                 sums[1, start : start + CH, :] = values[c]
+        if b == SENT_AFTER:
+            for side in range(2):
+                esend[1, side] = edges((gpl,), side)
+            beside, corners, row_copies = exchange(1, (gpl,))
     arrivals = [None, send_to_core(1)]
     z_copies = [None, None]
     for b in range(3):
@@ -420,11 +441,12 @@
 
     own_rows(gpl, 2)
     z_copies[0] = send_along_z(0, arrivals[0])
-    for copy in corners + row_copies[0]:
+    for copy in beside + corners + row_copies[0]:
         copy.wait_recv()
-    finish_rows(1, 0, 2)
+    finish_own(1, 0, 2)
+    outer_rows(1, 0, 2)
     for hp in range(pairs):
-        spread(gi_ref, hp, conv(2, hp, w3, True).astype(BF16))
+        spread(gi_ref, hp, conv(2, hp, w3, True, range(4)).astype(BF16))
 
     starts = [(k * rows_first) // n_wa for k in range(n_wa)]
     span = window.shape[3]
@@ -493,7 +515,7 @@
     exact = (TAPS * CH * CH) // (n_ha * n_wa)
     out_rows = -(-exact // 128)
     span = round_up(out_rows + 1, 8)
-    first_pad = round_up(max(rows_first, (n_wa - 1) * rows_first // n_wa + span), 16)
+    first_pad = round_up(max(rows_first, (n_wa - 1) * rows_first // n_wa + span), 8)
     any_spec = pl.BlockSpec(memory_space=pl.ANY)
     vmem_spec = pl.BlockSpec(memory_space=pltpu.VMEM)
     dma = pltpu.SemaphoreType.DMA
@@ -518,7 +540,7 @@
             pltpu.VMEM((3, 2, cols, LANES), BF16),
             pltpu.VMEM((3, 3, rows + 2, cols, PADDED), BF16),
             pltpu.VMEM((rows, cols, LANES), BF16),
-            pltpu.VMEM((rows // 2, cols * DEPTH // 2, PATCH), F32),
+            pltpu.VMEM((2, rows // 2, cols * DEPTH // 2, PATCH), F32),
             pltpu.VMEM((2, PATCH, rows * cols * 2), BF16),
             pltpu.VMEM((2, TAPS * CH, PAIR), F32),
             pltpu.VMEM((2, 2, n_ha // 2, first_pad, 128), BF16),

time: 32.9 us -> 31.9 us (0.970); the launches traced: 32.6 us -> 31.3 us
  Pallas kernels: 32 us -> 30.6 us
    pallas_call x1, Pallas kernels: 30.7 us -> 29.3 us  [shards(): pl.pallas_call(functools.partial(kernel, sizes), out_shape=(pltpu.VMEM((r...]
where the time goes in v3:
time: 31.9 us; the launch traced here: 31.3 us
  Pallas kernels  30.6 us (96%)
  between operations  0.64 us (2%)
    pallas_call x1, Pallas kernels, shards(): pl.pallas_call(functools.partial(kernel, sizes), out_shape=(pltpu.VMEM((r...  29.3 us
    pallas_call x1, Pallas kernels, shards(): pl.pallas_call(functools.partial(finish, sizes), out_shape=(jax.ShapeDtyp...  1.3 us

profile of v3, /device:TPU:1, one launch (start us, length us, event | category | flops | bytes accessed | tf_op | source)
XLA Modules:
  0.0 31.3 jit_solution(1279321007818340944)
XLA Ops:
  0.6 29.3 %shard_map.67 = (bf16[4,64,512]{2,1,0:T(8,128)(2,1)S(1)}, f32[2,8,128]{2,1,0:T(8,128)S(1)}) custom-call(bf16[4,64,512]{2,1,0:T(8,128)(2,1)} %x_hbm.1, bf16[4,64,512]{2,1,0:T(8,128)(2,1)} %g_hbm.1, bf16[27,64,64]{2,1,0:T(8,128)(2,1)} %k1_hbm.1, bf16[27,64,64]{2,1,0:T(8,128)(2,1)} %k2_hbm.1), custom_call_target="tpu_custom_call" | custom-call | tf_op jit(solution)/shard_map/pallas_call | solution.py:522
  30.0 1.3 %shard_map.68 = (bf16[4,64,512]{2,1,0:T(8,128)(2,1)}, f32[864]{0:T(1024)}, f32[864]{0:T(1024)}) custom-call(bf16[4,64,512]{2,1,0:T(8,128)(2,1)S(1)} %get-tuple-element.5.gi_ref, f32[2,8,128]{2,1,0:T(8,128)S(1)} %get-tuple-element.6.fin_ref), custom_call_target="tpu_custom_call" | custom-call | tf_op jit(solution)/shard_map/pallas_call | solution.py:567

commit v4 on v3

--- a/solution.py
+++ b/solution.py
@@ -53,8 +53,6 @@
     sums,
     piece,
     got,
-    along,
-    along_got,
     total,
     window,
     wgot,
@@ -63,8 +61,6 @@
     halo_recv,
     core_send,
     core_recv,
-    z_send,
-    z_recv,
     last_send,
     last_recv,
 ):
@@ -90,15 +86,21 @@
     upper = lax.rem(lax.div(ha, 2), 2)
     z_here = lax.div(ha, 4)
     other_core = ha + 1 - 2 * core
-    other_upper = ha + 2 - 4 * upper
 
     barrier = pltpu.get_barrier_semaphore()
     peers = [(ha_at(a), wa) for a in (-1, 1)]
     peers += [(ha, wa_at(d)) for d in (-1, 1)[: n_wa - 1]]
     peers += [(ha_at(a), wa_at(b)) for a in (-1, 1) for b in (-1, 1)]
-    peers += [(ha, wa_at(d)) for d in range(2, n_wa - 1)]
-    peers += [(other_upper, wa_at(d)) for d in range(n_wa)]
-    peers += [(ha_at(4 * d), wa) for d in range(1, n_z)]
+    chips = []
+    for dz in range(n_z):
+        for du in range(2):
+            for dw in range(n_wa):
+                if dz + du + dw:
+                    to_z = wrap(z_here + dz, n_z)
+                    to_u = upper if du == 0 else 1 - upper
+                    chips.append(((to_z, to_u, wa_at(dw)), (to_z * 4 + to_u * 2 + core, wa_at(dw))))
+                    if dz + du or 1 < dw < n_wa - 1:
+                        peers.append(chips[-1][1])
     loads = [
         pltpu.make_async_copy(x_hbm, xl, local_sem.at[2]),
         pltpu.make_async_copy(g_hbm, gl, local_sem.at[3]),
@@ -393,20 +395,26 @@
         sent.append(copy)
         return copy
 
-    def send_along_z(which, arrival):
+    starts = [(k * rows_first) // n_wa for k in range(n_wa)]
+    span = window.shape[4]
+
+    def send_to_chips(which, arrival):
         arrival.wait_recv()
         for t in range(n_ha // 2):
-            value = piece[which, core, t].astype(F32) + got[which, t].astype(F32)
-            along[which, t // 2, t % 2] = value.astype(BF16)
+            total[t] = piece[which, core, t].astype(F32) + got[which, t].astype(F32)
+        for t in range(n_ha // 2):
+            for k in range(n_wa):
+                value = total[t, starts[k] : starts[k] + span, :]
+                window[which, t // 2, t % 2, k] = value.astype(BF16)
         copies = []
-        for d in range(1, n_z):
+        for i, ((to_z, to_u, to_w), peer) in enumerate(chips):
             copies.append(
                 pltpu.make_async_remote_copy(
-                    src_ref=along.at[which, wrap(z_here + d, n_z)],
-                    dst_ref=along_got.at[which, d],
-                    send_sem=z_send.at[which, d],
-                    recv_sem=z_recv.at[which, d],
-                    device_id=(ha_at(4 * d), wa),
+                    src_ref=window.at[which, to_z, to_u, to_w],
+                    dst_ref=wgot.at[which, i],
+                    send_sem=last_send.at[which, i],
+                    recv_sem=last_recv.at[which, i],
+                    device_id=peer,
                     device_id_type=MESH,
                 )
             )
@@ -427,7 +435,7 @@
                 esend[1, side] = edges((gpl,), side)
             beside, corners, row_copies = exchange(1, (gpl,))
     arrivals = [None, send_to_core(1)]
-    z_copies = [None, None]
+    lasts = [None, None]
     for b in range(3):
         for a, even0, even1, odd0, odd1 in gradients(0, b):
             turn = pltpu.roll(odd1, CH, 1)
@@ -435,12 +443,11 @@
             start = (9 * a + 3 * b) * CH
             sums[0, start : start + 2 * CH, 0:CH] = both.T
             sums[0, start + 2 * CH : start + 3 * CH, 0:CH] = (even1 + turn).T[0:CH]
-        if b == 1:
-            z_copies[1] = send_along_z(1, arrivals[1])
     arrivals[0] = send_to_core(0)
 
+    lasts[1] = send_to_chips(1, arrivals[1])
+    lasts[0] = send_to_chips(0, arrivals[0])
     own_rows(gpl, 2)
-    z_copies[0] = send_along_z(0, arrivals[0])
     for copy in beside + corners + row_copies[0]:
         copy.wait_recv()
     finish_own(1, 0, 2)
@@ -448,46 +455,12 @@
     for hp in range(pairs):
         spread(gi_ref, hp, conv(2, hp, w3, True, range(4)).astype(BF16))
 
-    starts = [(k * rows_first) // n_wa for k in range(n_wa)]
-    span = window.shape[3]
     for which in (1, 0):
-        for copy in z_copies[which]:
+        value = window[which, z_here, upper, wa].astype(F32)
+        for copy in lasts[which]:
             copy.wait_recv()
-        for u in range(2):
-            value = along[which, z_here, u].astype(F32)
-            for d in range(1, n_z):
-                value += along_got[which, d, u].astype(F32)
-            total[which, u] = value
-            for k in range(n_wa):
-                window[u, k, which] = total[which, u, starts[k] : starts[k] + span, :]
-    lasts = []
-    for step in range(2):
-        up = upper if step == 0 else 1 - upper
-        for d in range(n_wa):
-            if step == 0 and d == 0:
-                continue
-            to = wa_at(d)
-            lasts.append(
-                pltpu.make_async_remote_copy(
-                    src_ref=window.at[up, to],
-                    dst_ref=wgot.at[step, d],
-                    send_sem=last_send.at[step, d],
-                    recv_sem=last_recv.at[step, d],
-                    device_id=(ha if step == 0 else other_upper, to),
-                    device_id_type=MESH,
-                )
-            )
-    for copy in lasts:
-        copy.start()
-    for copy in lasts:
-        copy.wait_recv()
-    value = window[upper, wa]
-    for step in range(2):
-        for d in range(n_wa):
-            if step or d:
-                value += wgot[step, d]
-    fin_ref[...] = value
-    for copy in sent + lasts:
+        fin_ref[which] = value + jnp.sum(wgot[which].astype(F32), axis=0)
+    for copy in sent:
         copy.wait_send()
 
 
@@ -545,20 +518,16 @@
             pltpu.VMEM((2, TAPS * CH, PAIR), F32),
             pltpu.VMEM((2, 2, n_ha // 2, first_pad, 128), BF16),
             pltpu.VMEM((2, n_ha // 2, first_pad, 128), BF16),
-            pltpu.VMEM((2, n_ha // 4, 2, first_pad, 128), BF16),
-            pltpu.VMEM((2, n_ha // 4, 2, first_pad, 128), BF16),
-            pltpu.VMEM((2, 2, first_pad, 128), F32),
-            pltpu.VMEM((2, n_wa, 2, span, 128), F32),
-            pltpu.VMEM((2, n_wa, 2, span, 128), F32),
+            pltpu.VMEM((n_ha // 2, first_pad, 128), F32),
+            pltpu.VMEM((2, n_ha // 4, 2, n_wa, span, 128), BF16),
+            pltpu.VMEM((2, n_ha // 2 * n_wa - 1, span, 128), BF16),
             dma((4,)),
             dma((2, 10)),
             dma((2, 10)),
             dma((2,)),
             dma((2,)),
-            dma((2, n_ha // 4)),
-            dma((2, n_ha // 4)),
-            dma((2, n_wa)),
-            dma((2, n_wa)),
+            dma((2, n_ha // 2 * n_wa - 1)),
+            dma((2, n_ha // 2 * n_wa - 1)),
         ],
         compiler_params=pltpu.CompilerParams(
             collective_id=0, has_side_effects=True, vmem_limit_bytes=65024 * 1024

time: 31.9 us -> 32.3 us (1.013); the launches traced: 31.3 us -> 32.2 us
  Pallas kernels: 30.6 us -> 31.5 us
    pallas_call x1, Pallas kernels: 29.3 us -> 30.3 us  [shards(): pl.pallas_call(functools.partial(kernel, sizes), out_shape=(pltpu.VMEM((r...]
where the time goes in v4:
time: 32.3 us; the launch traced here: 32.2 us
  Pallas kernels  31.5 us (98%)
  between operations  0.64 us (2%)
    pallas_call x1, Pallas kernels, shards(): pl.pallas_call(functools.partial(kernel, sizes), out_shape=(pltpu.VMEM((r...  30.3 us
    pallas_call x1, Pallas kernels, shards(): pl.pallas_call(functools.partial(finish, sizes), out_shape=(jax.ShapeDtyp...  1.3 us

profile of v4, /device:TPU:1, one launch (start us, length us, event | category | flops | bytes accessed | tf_op | source)
XLA Modules:
  0.0 32.2 jit_solution(4097673409548611954)
XLA Ops:
  0.6 30.3 %shard_map.67 = (bf16[4,64,512]{2,1,0:T(8,128)(2,1)S(1)}, f32[2,8,128]{2,1,0:T(8,128)S(1)}) custom-call(bf16[4,64,512]{2,1,0:T(8,128)(2,1)} %x_hbm.1, bf16[4,64,512]{2,1,0:T(8,128)(2,1)} %g_hbm.1, bf16[27,64,64]{2,1,0:T(8,128)(2,1)} %k1_hbm.1, bf16[27,64,64]{2,1,0:T(8,128)(2,1)} %k2_hbm.1), custom_call_target="tpu_custom_call" | custom-call | tf_op jit(solution)/shard_map/pallas_call | solution.py:495
  30.9 1.3 %shard_map.68 = (bf16[4,64,512]{2,1,0:T(8,128)(2,1)}, f32[864]{0:T(1024)}, f32[864]{0:T(1024)}) custom-call(bf16[4,64,512]{2,1,0:T(8,128)(2,1)S(1)} %get-tuple-element.5.gi_ref, f32[2,8,128]{2,1,0:T(8,128)S(1)} %get-tuple-element.6.fin_ref), custom_call_target="tpu_custom_call" | custom-call | tf_op jit(solution)/shard_map/pallas_call | solution.py:536

commit v5 on v4

--- a/solution.py
+++ b/solution.py
@@ -398,22 +398,24 @@
     starts = [(k * rows_first) // n_wa for k in range(n_wa)]
     span = window.shape[4]
 
-    def send_to_chips(which, arrival):
+    def merge_cores(which, arrival):
         arrival.wait_recv()
         for t in range(n_ha // 2):
             total[t] = piece[which, core, t].astype(F32) + got[which, t].astype(F32)
         for t in range(n_ha // 2):
             for k in range(n_wa):
                 value = total[t, starts[k] : starts[k] + span, :]
-                window[which, t // 2, t % 2, k] = value.astype(BF16)
+                window[t // 2, t % 2, k, which] = value.astype(BF16)
+
+    def send_to_chips():
         copies = []
         for i, ((to_z, to_u, to_w), peer) in enumerate(chips):
             copies.append(
                 pltpu.make_async_remote_copy(
-                    src_ref=window.at[which, to_z, to_u, to_w],
-                    dst_ref=wgot.at[which, i],
-                    send_sem=last_send.at[which, i],
-                    recv_sem=last_recv.at[which, i],
+                    src_ref=window.at[to_z, to_u, to_w],
+                    dst_ref=wgot.at[i],
+                    send_sem=last_send.at[i],
+                    recv_sem=last_recv.at[i],
                     device_id=peer,
                     device_id_type=MESH,
                 )
@@ -435,7 +437,6 @@
                 esend[1, side] = edges((gpl,), side)
             beside, corners, row_copies = exchange(1, (gpl,))
     arrivals = [None, send_to_core(1)]
-    lasts = [None, None]
     for b in range(3):
         for a, even0, even1, odd0, odd1 in gradients(0, b):
             turn = pltpu.roll(odd1, CH, 1)
@@ -445,8 +446,9 @@
             sums[0, start + 2 * CH : start + 3 * CH, 0:CH] = (even1 + turn).T[0:CH]
     arrivals[0] = send_to_core(0)
 
-    lasts[1] = send_to_chips(1, arrivals[1])
-    lasts[0] = send_to_chips(0, arrivals[0])
+    merge_cores(1, arrivals[1])
+    merge_cores(0, arrivals[0])
+    lasts = send_to_chips()
     own_rows(gpl, 2)
     for copy in beside + corners + row_copies[0]:
         copy.wait_recv()
@@ -455,11 +457,10 @@
     for hp in range(pairs):
         spread(gi_ref, hp, conv(2, hp, w3, True, range(4)).astype(BF16))
 
-    for which in (1, 0):
-        value = window[which, z_here, upper, wa].astype(F32)
-        for copy in lasts[which]:
-            copy.wait_recv()
-        fin_ref[which] = value + jnp.sum(wgot[which].astype(F32), axis=0)
+    value = window[z_here, upper, wa].astype(F32)
+    for copy in lasts:
+        copy.wait_recv()
+    fin_ref[...] = value + jnp.sum(wgot[...].astype(F32), axis=0)
     for copy in sent:
         copy.wait_send()
 
@@ -519,15 +520,15 @@
             pltpu.VMEM((2, 2, n_ha // 2, first_pad, 128), BF16),
             pltpu.VMEM((2, n_ha // 2, first_pad, 128), BF16),
             pltpu.VMEM((n_ha // 2, first_pad, 128), F32),
-            pltpu.VMEM((2, n_ha // 4, 2, n_wa, span, 128), BF16),
-            pltpu.VMEM((2, n_ha // 2 * n_wa - 1, span, 128), BF16),
+            pltpu.VMEM((n_ha // 4, 2, n_wa, 2, span, 128), BF16),
+            pltpu.VMEM((n_ha // 2 * n_wa - 1, 2, span, 128), BF16),
             dma((4,)),
             dma((2, 10)),
             dma((2, 10)),
             dma((2,)),
             dma((2,)),
-            dma((2, n_ha // 2 * n_wa - 1)),
-            dma((2, n_ha // 2 * n_wa - 1)),
+            dma((n_ha // 2 * n_wa - 1,)),
+            dma((n_ha // 2 * n_wa - 1,)),
         ],
         compiler_params=pltpu.CompilerParams(
             collective_id=0, has_side_effects=True, vmem_limit_bytes=65024 * 1024

time: 32.3 us -> 31 us (0.960)
  Pallas kernels: 31.5 us -> 30.3 us
    pallas_call x1, Pallas kernels: 30.3 us -> 29 us  [shards(): pl.pallas_call(functools.partial(kernel, sizes), out_shape=(pltpu.VMEM((r...]
where the time goes in v5:
time: 31 us; the launch traced here: 30.9 us
  Pallas kernels  30.3 us (98%)
  between operations  0.64 us (2%)
    pallas_call x1, Pallas kernels, shards(): pl.pallas_call(functools.partial(kernel, sizes), out_shape=(pltpu.VMEM((r...  29 us
    pallas_call x1, Pallas kernels, shards(): pl.pallas_call(functools.partial(finish, sizes), out_shape=(jax.ShapeDtyp...  1.3 us

profile of v5, /device:TPU:1, one launch (start us, length us, event | category | flops | bytes accessed | tf_op | source)
XLA Modules:
  0.0 30.9 jit_solution(10226310539530413927)
XLA Ops:
  0.6 29.0 %shard_map.67 = (bf16[4,64,512]{2,1,0:T(8,128)(2,1)S(1)}, f32[2,8,128]{2,1,0:T(8,128)S(1)}) custom-call(bf16[4,64,512]{2,1,0:T(8,128)(2,1)} %x_hbm.1, bf16[4,64,512]{2,1,0:T(8,128)(2,1)} %g_hbm.1, bf16[27,64,64]{2,1,0:T(8,128)(2,1)} %k1_hbm.1, bf16[27,64,64]{2,1,0:T(8,128)(2,1)} %k2_hbm.1), custom_call_target="tpu_custom_call" | custom-call | tf_op jit(solution)/shard_map/pallas_call | solution.py:496
  29.6 1.3 %shard_map.68 = (bf16[4,64,512]{2,1,0:T(8,128)(2,1)}, f32[864]{0:T(1024)}, f32[864]{0:T(1024)}) custom-call(bf16[4,64,512]{2,1,0:T(8,128)(2,1)S(1)} %get-tuple-element.5.gi_ref, f32[2,8,128]{2,1,0:T(8,128)S(1)} %get-tuple-element.6.fin_ref), custom_call_target="tpu_custom_call" | custom-call | tf_op jit(solution)/shard_map/pallas_call | solution.py:537

commit v6 on v5

--- a/solution.py
+++ b/solution.py
@@ -16,7 +16,7 @@
 PATCH = 4 * CH
 KTOTAL = 3 * 16 * CH
 MESH = pl.DeviceIdType.MESH
-SENT_AFTER = 0
+SENT_AFTER = 2
 F32 = jnp.float32
 BF16 = jnp.bfloat16
 
@@ -98,9 +98,12 @@
                 if dz + du + dw:
                     to_z = wrap(z_here + dz, n_z)
                     to_u = upper if du == 0 else 1 - upper
-                    chips.append(((to_z, to_u, wa_at(dw)), (to_z * 4 + to_u * 2 + core, wa_at(dw))))
+                    far = min(dz, n_z - dz) + 2 * du + min(dw, n_wa - dw)
+                    peer = (to_z * 4 + to_u * 2 + core, wa_at(dw))
+                    chips.append((-far, (to_z, to_u, wa_at(dw)), peer))
                     if dz + du or 1 < dw < n_wa - 1:
-                        peers.append(chips[-1][1])
+                        peers.append(peer)
+    chips = [entry[1:] for entry in sorted(chips, key=lambda entry: entry[0])]
     loads = [
         pltpu.make_async_copy(x_hbm, xl, local_sem.at[2]),
         pltpu.make_async_copy(g_hbm, gl, local_sem.at[3]),
@@ -465,12 +468,11 @@
         copy.wait_send()
 
 
-def finish(sizes, gi_ref, fin_ref, gi_hbm, one_ref, two_ref, sem):
+def finish(sizes, gi_ref, fin_ref, gi_out, one_ref, two_ref):
     n_ha, n_wa, rows, cols = sizes
     wa = lax.axis_index("wa")
     exact = (TAPS * CH * CH) // (n_ha * n_wa)
-    store = pltpu.make_async_copy(gi_ref, gi_hbm, sem)
-    store.start()
+    gi_out[...] = gi_ref[...]
     offset = lax.rem(wa * exact, 128)
     count = -(-exact // 128)
     lanes = lax.broadcasted_iota(jnp.int32, (count, 128), 1)
@@ -480,7 +482,6 @@
         for r in range(count):
             width = min(128, exact - r * 128)
             out[pl.ds(r * 128, width)] = value[r, 0:width]
-    store.wait()
 
 
 def shards(sizes, inputs, grad_out, kernel_one, kernel_two):
@@ -542,8 +543,7 @@
             jax.ShapeDtypeStruct((exact,), F32),
         ),
         in_specs=[vmem_spec, vmem_spec],
-        out_specs=(any_spec, vmem_spec, vmem_spec),
-        scratch_shapes=[dma],
+        out_specs=(vmem_spec, vmem_spec, vmem_spec),
         compiler_params=pltpu.CompilerParams(vmem_limit_bytes=8 * 1024 * 1024),
     )(grad_inputs, fin)
 

time: 31 us -> 30.4 us (0.981)
  Pallas kernels: 30.3 us -> 29.6 us
    pallas_call x1, Pallas kernels: 1.3 us -> 0.72 us  [shards(): pl.pallas_call(functools.partial(finish, sizes), out_shape=(jax.ShapeDtyp...]
where the time goes in v6:
time: 30.4 us; the launch traced here: 30.2 us
  Pallas kernels  29.6 us (97%)
  between operations  0.64 us (2%)
    pallas_call x1, Pallas kernels, shards(): pl.pallas_call(functools.partial(kernel, sizes), out_shape=(pltpu.VMEM((r...  28.9 us
    pallas_call x1, Pallas kernels, shards(): pl.pallas_call(functools.partial(finish, sizes), out_shape=(jax.ShapeDtyp...  0.72 us

profile of v6, /device:TPU:1, one launch (start us, length us, event | category | flops | bytes accessed | tf_op | source)
XLA Modules:
  0.0 30.2 jit_solution(5424962762026130748)
XLA Ops:
  0.6 28.9 %shard_map.67 = (bf16[4,64,512]{2,1,0:T(8,128)(2,1)S(1)}, f32[2,8,128]{2,1,0:T(8,128)S(1)}) custom-call(bf16[4,64,512]{2,1,0:T(8,128)(2,1)} %x_hbm.1, bf16[4,64,512]{2,1,0:T(8,128)(2,1)} %g_hbm.1, bf16[27,64,64]{2,1,0:T(8,128)(2,1)} %k1_hbm.1, bf16[27,64,64]{2,1,0:T(8,128)(2,1)} %k2_hbm.1), custom_call_target="tpu_custom_call" | custom-call | tf_op jit(solution)/shard_map/pallas_call | solution.py:497
  29.5 0.7 %shard_map.68 = (bf16[4,64,512]{2,1,0:T(8,128)(2,1)}, f32[864]{0:T(1024)}, f32[864]{0:T(1024)}) custom-call(bf16[4,64,512]{2,1,0:T(8,128)(2,1)S(1)} %get-tuple-element.5.gi_ref, f32[2,8,128]{2,1,0:T(8,128)S(1)} %get-tuple-element.6.fin_ref), custom_call_target="tpu_custom_call" | custom-call | tf_op jit(solution)/shard_map/pallas_call | solution.py:538

commit v7 on v6

--- a/solution.py
+++ b/solution.py
@@ -121,13 +121,13 @@
 
     def edges(field_refs, side):
         start, pick = (0, 0) if side == 0 else (cols - 16, 15)
-        ids = lax.broadcasted_iota(jnp.int32, (16, LANES), 0)
-        value = jnp.zeros((16, LANES), F32)
+        ids = lax.broadcasted_iota(jnp.int32, (2 * rows, LANES), 0)
+        value = jnp.zeros((2 * rows, LANES), F32)
         for f, ref in enumerate(field_refs):
             for h in range(rows):
                 block = ref[h, start : start + 16, :].astype(F32)
-                cell = jnp.broadcast_to(block[pick : pick + 1], (16, LANES))
-                value = jnp.where(ids == f * 8 + h, cell, value)
+                cell = jnp.broadcast_to(block[pick : pick + 1], (2 * rows, LANES))
+                value = jnp.where(ids == f * rows + h, cell, value)
         return value.astype(BF16)
 
     def exchange(phase, field_refs):
@@ -196,8 +196,8 @@
     def finish_own(phase, f, dst):
         sides = [halo_cells(phase, side, 1) for side in range(2)]
         for h in range(rows):
-            left = sides[0][f * 8 + h : f * 8 + h + 1]
-            right = sides[1][f * 8 + h : f * 8 + h + 1]
+            left = sides[0][f * rows + h : f * rows + h + 1]
+            right = sides[1][f * rows + h : f * rows + h + 1]
             tile = shifted[dst, 0, h + 1, 0:16, :].astype(F32)
             tile = jnp.where(tile_ids == 0, jnp.broadcast_to(left, (16, PADDED)), tile)
             shifted[dst, 0, h + 1, 0:16, :] = tile.astype(BF16)
@@ -209,8 +209,8 @@
         slot = phase * 2 + f
         for e, side, ok, r, h in ((0, 0, low_ok, 0, rows - 1), (rows + 1, 1, high_ok, 2, 0)):
             value = widen(jnp.where(ok, rowbuf[slot, side].astype(F32), 0.0))
-            left = halo_cells(phase, 0, r)[f * 8 + h : f * 8 + h + 1]
-            right = halo_cells(phase, 1, r)[f * 8 + h : f * 8 + h + 1]
+            left = halo_cells(phase, 0, r)[f * rows + h : f * rows + h + 1]
+            right = halo_cells(phase, 1, r)[f * rows + h : f * rows + h + 1]
             before = jnp.where(
                 cell_ids == 0,
                 jnp.broadcast_to(left, (cols, PADDED)),
@@ -461,11 +461,11 @@
         spread(gi_ref, hp, conv(2, hp, w3, True, range(4)).astype(BF16))
 
     value = window[z_here, upper, wa].astype(F32)
+    for copy in sent:
+        copy.wait_send()
     for copy in lasts:
         copy.wait_recv()
     fin_ref[...] = value + jnp.sum(wgot[...].astype(F32), axis=0)
-    for copy in sent:
-        copy.wait_send()
 
 
 def finish(sizes, gi_ref, fin_ref, gi_out, one_ref, two_ref):
@@ -510,8 +510,8 @@
             pltpu.VMEM((KTOTAL, PATCH), BF16),
             pltpu.VMEM((PATCH, KTOTAL), BF16),
             pltpu.VMEM((PATCH, KTOTAL), BF16),
-            pltpu.VMEM((2, 2, 16, LANES), BF16),
-            pltpu.VMEM((2, 6, 16, LANES), BF16),
+            pltpu.VMEM((2, 2, 2 * rows, LANES), BF16),
+            pltpu.VMEM((2, 6, 2 * rows, LANES), BF16),
             pltpu.VMEM((3, 2, cols, LANES), BF16),
             pltpu.VMEM((3, 3, rows + 2, cols, PADDED), BF16),
             pltpu.VMEM((rows, cols, LANES), BF16),

time: 30.4 us -> 29.9 us (0.984)
  Pallas kernels: 29.6 us -> 29.2 us
    pallas_call x1, Pallas kernels: 28.9 us -> 28.4 us  [shards(): pl.pallas_call(functools.partial(kernel, sizes), out_shape=(pltpu.VMEM((r...]
where the time goes in v7:
time: 29.9 us; the launch traced here: 29.8 us
  Pallas kernels  29.2 us (98%)
  between operations  0.64 us (2%)
    pallas_call x1, Pallas kernels, shards(): pl.pallas_call(functools.partial(kernel, sizes), out_shape=(pltpu.VMEM((r...  28.4 us
    pallas_call x1, Pallas kernels, shards(): pl.pallas_call(functools.partial(finish, sizes), out_shape=(jax.ShapeDtyp...  0.72 us

profile of v7, /device:TPU:1, one launch (start us, length us, event | category | flops | bytes accessed | tf_op | source)
XLA Modules:
  0.0 29.8 jit_solution(13733707780900716887)
XLA Ops:
  0.6 28.4 %shard_map.67 = (bf16[4,64,512]{2,1,0:T(8,128)(2,1)S(1)}, f32[2,8,128]{2,1,0:T(8,128)S(1)}) custom-call(bf16[4,64,512]{2,1,0:T(8,128)(2,1)} %x_hbm.1, bf16[4,64,512]{2,1,0:T(8,128)(2,1)} %g_hbm.1, bf16[27,64,64]{2,1,0:T(8,128)(2,1)} %k1_hbm.1, bf16[27,64,64]{2,1,0:T(8,128)(2,1)} %k2_hbm.1), custom_call_target="tpu_custom_call" | custom-call | tf_op jit(solution)/shard_map/pallas_call | solution.py:497
  29.1 0.7 %shard_map.68 = (bf16[4,64,512]{2,1,0:T(8,128)(2,1)}, f32[864]{0:T(1024)}, f32[864]{0:T(1024)}) custom-call(bf16[4,64,512]{2,1,0:T(8,128)(2,1)S(1)} %get-tuple-element.5.gi_ref, f32[2,8,128]{2,1,0:T(8,128)S(1)} %get-tuple-element.6.fin_ref), custom_call_target="tpu_custom_call" | custom-call | tf_op jit(solution)/shard_map/pallas_call | solution.py:538
